TPU v7x, 32 devices: a whole 2x2x4 slice. The times are simulated.
32 devices in a mesh: groups: 2 (over x), seq: 16 (over z, y, core).
Axes of the slice: x: 2, y: 2, z: 4, core: 2. Of those that a mesh axis runs over, the one named last changes fastest.
Arguments:
- query_in: bfloat16 [4096, 4096], P(('groups', 'seq')), parts along dimension 0, may hold values from -6 to 6
- key_in: bfloat16 [4096, 4096], P(('groups', 'seq')), parts along dimension 0, may hold values from -6 to 6
- value_in: bfloat16 [4096, 4096], P(('groups', 'seq')), parts along dimension 0, may hold values from -6 to 6
- long_filter: bfloat16 [2048, 4096], P('seq'), may hold values from -0.4 to 0.4
- short_weight: float32 [3, 3, 4096], replicated, may hold values from -3 to 3
- skip_gain: float32 [4096], replicated, may hold values from 0.5 to 1.5
Outputs:
- gated_out: bfloat16 [4096, 4096], P(('groups', 'seq')), parts along dimension 0
There are 2 independent parts, one for each index of `groups`. A program takes and returns all parts, laid end to end along the dimension named above; an argument that names none is the same for every part. Nothing has to cross between parts.
All inputs are finite; a program needn't handle non-finite values.
Results may differ from a plain program's by a relative error of at most 0.0052.
Values may be sent and summed in bfloat16 or wider, within the bound.
No kernel may reach another device: no remote copies, remote signals or barrier semaphores. Data moves between devices by JAX's collectives and lax.ppermute only.
A program may use at most 128 MiB of HBM per device.

v0:
```python
import math
import jax
import jax.numpy as jnp
from jax import lax
from jax.sharding import PartitionSpec as P

PRECISE = lax.Precision.HIGHEST


def from_behind(value, axis, steps):
    count = lax.axis_size(axis)
    initial, last = (max(0, -steps), min(count, count - steps))
    return lax.ppermute(value, axis, [(source, source + steps) for source in range(initial, last)])


def featurize(own_rows, earlier, taps_weight):
    rim_rows = earlier.shape[0]
    row_count = own_rows.shape[0]
    extended = jnp.concatenate([earlier, own_rows], axis=0).astype(jnp.float32)
    result = jnp.zeros(own_rows.shape, jnp.float32)
    for offset in range(rim_rows + 1):
        result = (
            result
            + taps_weight[offset] * extended[rim_rows - offset : rim_rows - offset + row_count]
        )
    return result


def phase_pair(left_index, right_index, modulus):
    product_index = left_index[:, None] * right_index[None, :] % modulus
    angle = product_index.astype(jnp.float32) * (2.0 * math.pi / modulus)
    return (jnp.cos(angle), jnp.sin(angle))


def block_forward(real_blocks):
    blocks = real_blocks.shape[0]
    flat_values = real_blocks.reshape(blocks, -1)
    cosine_table, sine_table = phase_pair(
        jnp.arange(2 * blocks, dtype=jnp.int32), jnp.arange(blocks, dtype=jnp.int32), 2 * blocks
    )
    joint_table = jnp.concatenate([cosine_table, -sine_table], axis=0)
    stacked = jnp.dot(joint_table, flat_values, precision=PRECISE)
    return stacked.reshape((2, 2 * blocks) + real_blocks.shape[1:])


def apply_twiddle(stacked, freq_index, row_index, modulus, direction):
    cosine_table, sine_table = phase_pair(freq_index, row_index, modulus)
    cosine_table = cosine_table[:, :, None]
    sine_table = direction * sine_table[:, :, None]
    out_real = stacked[0] * cosine_table + stacked[1] * sine_table
    out_imaginary = stacked[1] * cosine_table - stacked[0] * sine_table
    return jnp.stack([out_real, out_imaginary])


def row_transform(stacked, direction):
    length = stacked.shape[2]
    row_index = jnp.arange(length, dtype=jnp.int32)
    cosine_table, sine_table = phase_pair(row_index, row_index, length)
    sine_table = direction * sine_table
    upper_table = jnp.stack([cosine_table, sine_table], axis=1)
    lower_table = jnp.stack([-sine_table, cosine_table], axis=1)
    full_table = jnp.stack([upper_table, lower_table])
    return jnp.einsum("ymxn,xknc->ykmc", full_table, stacked, precision=PRECISE)


def block_inverse(stacked, factor):
    double_count = stacked.shape[1]
    blocks = double_count // 2
    cosine_table, sine_table = phase_pair(
        jnp.arange(blocks, dtype=jnp.int32), jnp.arange(double_count, dtype=jnp.int32), double_count
    )
    joint_table = jnp.concatenate([cosine_table, -sine_table], axis=1)
    flat_values = stacked.reshape(2 * double_count, -1)
    result = jnp.dot(joint_table, flat_values, precision=PRECISE) * factor
    return result.reshape((blocks,) + stacked.shape[2:])


def spectral_product(stacked, width):
    spectra = row_transform(stacked, 1.0)
    data_real = spectra[0, ..., :width]
    kernel_real = spectra[0, ..., width:]
    data_imaginary = spectra[1, ..., :width]
    kernel_imaginary = spectra[1, ..., width:]
    joint = jnp.stack(
        [
            data_real * kernel_real - data_imaginary * kernel_imaginary,
            data_real * kernel_imaginary + data_imaginary * kernel_real,
        ]
    )
    return row_transform(joint, -1.0)


def along_rows(product, long_filter):
    blocks = lax.axis_size("seq")
    device_index = lax.axis_index("seq")
    row_count, channels = product.shape
    row_share = row_count // blocks
    full_length = 2 * blocks * row_count
    data_parts, kernel_parts = (
        lax.all_to_all(
            product.reshape(1, row_count, channels), "seq", split_axis=1, concat_axis=0, tiled=True
        ),
        lax.all_to_all(
            long_filter.reshape(1, row_count, channels),
            "seq",
            split_axis=1,
            concat_axis=0,
            tiled=True,
        ),
    )
    joined = jnp.concatenate([data_parts, kernel_parts], axis=2).astype(jnp.float32)
    freq_all = jnp.arange(2 * blocks, dtype=jnp.int32)
    local_rows = device_index * row_share + jnp.arange(row_share, dtype=jnp.int32)
    spectra = apply_twiddle(block_forward(joined), freq_all, local_rows, full_length, 1.0)
    spectra = lax.all_to_all(spectra, "seq", split_axis=1, concat_axis=2, tiled=True)
    joint = spectral_product(spectra, channels)
    own_freq = device_index * 2 + jnp.arange(2, dtype=jnp.int32)
    whole_rows = jnp.arange(row_count, dtype=jnp.int32)
    joint = apply_twiddle(joint, own_freq, whole_rows, full_length, -1.0)
    joint = lax.all_to_all(
        joint.astype(jnp.bfloat16), "seq", split_axis=2, concat_axis=1, tiled=True
    ).astype(joint.dtype)
    convolved = block_inverse(joint, 1.0 / full_length).astype(jnp.bfloat16)
    convolved = lax.all_to_all(convolved, "seq", split_axis=0, concat_axis=1, tiled=True)
    return convolved.reshape(row_count, channels)


def on_device(query_in, key_in, value_in, long_filter, short_weight, skip_gain):
    rim_rows = short_weight.shape[1] - 1
    last_rows = jnp.stack([query_in[-rim_rows:], key_in[-rim_rows:], value_in[-rim_rows:]])
    earlier = from_behind(last_rows, "seq", 1)
    q_short = featurize(query_in, earlier[0], short_weight[0])
    k_short = featurize(key_in, earlier[1], short_weight[1])
    v_short = featurize(value_in, earlier[2], short_weight[2])
    product = (k_short * v_short).astype(jnp.bfloat16)
    product_wide = lax.optimization_barrier(product).astype(jnp.float32)
    convolved = along_rows(product, long_filter)
    gated_out = q_short * (convolved.astype(jnp.float32) + skip_gain * product_wide)
    return gated_out.astype(jnp.bfloat16)


def solution(mesh):
    placed = (
        P(("groups", "seq"), None),
        P(("groups", "seq"), None),
        P(("groups", "seq"), None),
        P("seq", None),
        P(),
        P(),
    )
    return jax.shard_map(
        on_device, mesh=mesh, in_specs=placed, out_specs=P(("groups", "seq"), None), check_vma=False
    )
```

profile of v0, /device:TPU:9, one launch (start us, length us, event | category | flops | bytes accessed | tf_op | source)
XLA Modules:
  0.0 698.6 jit_solution(10720077850557271215)
XLA Ops:
  0.0 0.9 slice_bitcast_fusion.5
  0.9 0.9 slice_bitcast_fusion.3
  1.8 0.1 pad_maximum_fusion.7
  1.9 3.7 collective-permute-start
  5.6 3.6 copy.66
  9.2 0.0 copy-start.2
  9.2 0.5 broadcast.416
  9.7 7.0 %reduce = bf16[128,4096]{1,0:T(8,128)(2,1)S(1)} reduce(bf16[128,1,4096]{2,1,0:T(2,128)(2,1)S(1)} %bitcast.152, bf16[]{:T(256)} %broadcast.416), dimensions={1}, to_apply=%bitcast.138.reduce_sub_computation | reduce | bytes 2097154
  16.7 0.0 copy-start
  16.8 0.0 copy-start.1
  16.8 1.9 reshape.316
  18.7 5.7 all-to-all-start.1
  24.4 0.0 copy-done.2
  24.4 0.1 fusion.82
  24.5 0.0 collective-permute-done
  24.6 0.0 copy-done
  24.6 0.3 maximum_convert_fusion.1
  24.9 0.3 maximum_convert_fusion.2
  25.2 1.3 fusion.18
  26.5 2.4 copy.67
  28.9 8.0 %reduce.1 = bf16[128,4096]{1,0:T(8,128)(2,1)} reduce(bf16[128,1,4096]{2,1,0:T(2,128)(2,1)S(1)} %bitcast.154, bf16[]{:T(256)} %broadcast.416), dimensions={1}, to_apply=%bitcast.139.reduce_sub_computation | reduce | bytes 2097154
  36.9 2.9 reshape.318
  39.8 9.3 %all-to-all-done.1 = bf16[16,2,16384]{2,1,0:T(2,128)(2,1)} async-done(((bf16[16,2,16384]{2,1,0:T(2,128)(2,1)}), bf16[16,2,16384]{2,1,0:T(2,128)(2,1)}, u32[]{:S(2)}, u32[]{:S(2)}) %all-to-all-start.1) | async-done | bytes 1048608 | tf_op jit(solution)/shard_map/all_to_all | solution.py:103
  49.2 5.3 all-to-all-start
  54.5 0.1 sine_negate_fusion
  54.5 0.1 fusion.64
  54.6 4.3 reshape.317
  59.0 2.1 copy.64
  61.1 18.2 %all-to-all-done = bf16[16,2,16384]{2,1,0:T(2,128)(2,1)} async-done(((bf16[16,2,16384]{2,1,0:T(2,128)(2,1)}), bf16[16,2,16384]{2,1,0:T(2,128)(2,1)}, u32[]{:S(2)}, u32[]{:S(2)}) %all-to-all-start) | async-done | bytes 1048608 | tf_op jit(solution)/shard_map/all_to_all | solution.py:100
  79.3 4.3 reshape.319
  83.6 1.1 copy.65
  84.7 1.4 pad_maximum_fusion.2
  86.1 1.2 copy.46
  87.3 6.8 fusion.59
  94.1 6.5 fusion.81
  100.6 8.2 %copy.48 = f32[4,8,8,8192]{3,2,1,0:T(8,128)S(1)} copy(f32[4,8,8,8192]{3,1,2,0:T(8,128)} %bitcast.145) | data formatting | bytes 16777216
  108.8 8.2 %copy.47 = f32[4,8,8,8192]{3,2,1,0:T(8,128)S(1)} copy(f32[4,8,8,8192]{3,1,2,0:T(8,128)} %bitcast.144) | data formatting | bytes 16777216
  117.1 6.9 fusion.8
  124.0 11.5 %pad_maximum_fusion = f32[2,32,8,8192]{3,2,0,1:T(8,128)} fusion(f32[1,32,8,8192]{3,2,0,1:T(8,128)} %get-tuple-element.6, f32[1,32,8,8192]{3,2,0,1:T(8,128)} %get-tuple-element.5), kind=kLoop, calls=%fused_computation.2 | loop fusion | flops 4194304 | bytes 33554432 | tf_op jit(solution)/shard_map/stack | solution.py:52
  135.5 5.5 all-to-all-start.2
  141.0 0.3 fusion.43
  141.3 0.3 broadcast_multiply_fusion
  141.5 0.3 fusion.41
  141.9 0.1 fusion.76
  142.0 358.8 %all-to-all-done.2 = f32[2,32,8,8192]{3,2,0,1:T(8,128)} async-done(((f32[2,32,8,8192]{3,2,0,1:T(8,128)}), f32[2,32,8,8192]{3,2,0,1:T(8,128)}, u32[]{:S(2)}, u32[]{:S(2)}) %all-to-all-start.2) | async-done | bytes 16777248 | tf_op jit(solution)/shard_map/all_to_all | solution.py:115
  500.8 30.7 %fusion.3 = f32[2,2,128,8192]{2,3,0,1:T(8,128)S(1)} fusion(f32[1,128,2,128]{3,1,2,0:T(8,128)S(1)} %get-tuple-element.24, f32[1,128,2,128]{3,1,2,0:T(8,128)S(1)} %get-tuple-element.25, f32[2,2,16,8,8192]{4,3,0,1,2:T(8,128)} %bitcast.23), kind=kOutput, calls=%fused_computation.6 | convolution fusion | flops 12884967424 | bytes 33816576 | tf_op jit(solution)/shard_map/ymxn,xknc->ykmc/dot_general | solution.py:63
  531.5 1.1 multiply_subtract_fusion
  532.6 6.7 fusion.15
  539.3 1.1 add_convert_fusion
  540.4 2.4 pad_maximum_fusion.1
  542.8 11.2 %copy.34 = bf16[2,2,128,4096]{3,0,1,2:T(2,128)(2,1)} copy(bf16[2,2,128,4096]{2,3,0,1:T(8,128)(2,1)} %pad_maximum_fusion.1) | data formatting | bytes 8388608 | tf_op jit(solution)/shard_map/stack | solution.py:52
  554.0 7.4 %all-to-all-start.3 = ((bf16[2,2,128,4096]{3,0,1,2:T(2,128)(2,1)}), bf16[2,2,128,4096]{3,0,1,2:T(2,128)(2,1)}, u32[]{:S(2)}, u32[]{:S(2)}) async-start(bf16[2,2,128,4096]{3,0,1,2:T(2,128)(2,1)} %copy.34), calls=%async_computation.3 | async-start | bytes 8388608 | tf_op jit(solution)/shard_map/all_to_all | solution.py:120
  561.5 0.1 sine_negate_fusion.1
  561.5 90.1 %all-to-all-done.3 = bf16[2,2,128,4096]{3,0,1,2:T(2,128)(2,1)} async-done(((bf16[2,2,128,4096]{3,0,1,2:T(2,128)(2,1)}), bf16[2,2,128,4096]{3,0,1,2:T(2,128)(2,1)}, u32[]{:S(2)}, u32[]{:S(2)}) %all-to-all-start.3) | async-done | bytes 4194336 | tf_op jit(solution)/shard_map/all_to_all | solution.py:120
  651.6 5.1 copy.63
  656.7 0.5 copy.36
  657.2 2.6 copy.49
  659.8 1.8 fusion
  661.6 0.0 copy-start.3
  661.6 1.5 copy.50
  663.2 7.1 %all-to-all-start.4 = ((bf16[16,8,4096]{2,1,0:T(8,128)(2,1)}), bf16[16,8,4096]{2,1,0:T(8,128)(2,1)}, u32[]{:S(2)}, u32[]{:S(2)}) async-start(bf16[16,8,4096]{2,1,0:T(8,128)(2,1)} %bitcast.63), calls=%async_computation.4 | async-start | bytes 2097152 | tf_op jit(solution)/shard_map/all_to_all | solution.py:124
  670.3 1.5 maximum_convert_fusion
  671.8 23.4 %all-to-all-done.4 = bf16[16,8,4096]{2,1,0:T(8,128)(2,1)} async-done(((bf16[16,8,4096]{2,1,0:T(8,128)(2,1)}), bf16[16,8,4096]{2,1,0:T(8,128)(2,1)}, u32[]{:S(2)}, u32[]{:S(2)}) %all-to-all-start.4) | async-done | bytes 1048608 | tf_op jit(solution)/shard_map/all_to_all | solution.py:124
  695.2 3.2 fusion.24
  (6 shorter events, 0.1 us)
Async XLA Ops:
  1.9 22.6 %collective-permute-start = (bf16[3,2,4096]{2,1,0:T(2,128)(2,1)S(1)}, bf16[3,2,4096]{2,1,0:T(2,128)(2,1)S(1)}, u32[]{:S(2)}, u32[]{:S(2)}) collective-permute-start(bf16[3,2,4096]{2,1,0:T(2,128)(2,1)S(1)} %pad_maximum_fusion.7), channel_id=1, source_target_pairs={{0,1},{1,2},{2,3},{3,4},{4,5},{5,6},{6,7},{7,8},{8,9},{9,10},{10,1... | collective-permute-start | bytes 147464 | tf_op jit(solution)/shard_map/ppermute | solution.py:13
  9.2 15.2 %copy-start.2 = (f32[3,3,4096]{2,1,0:T(4,128)S(1)}, f32[3,3,4096]{2,1,0:T(4,128)}, u32[]{:S(2)}) copy-start(f32[3,3,4096]{2,1,0:T(4,128)} %param.10) | copy-start | bytes 442372
  16.7 7.8 %copy-start = (bf16[128,4096]{1,0:T(8,128)(2,1)S(1)}, bf16[128,4096]{1,0:T(8,128)(2,1)}, u32[]{:S(2)}) copy-start(bf16[128,4096]{1,0:T(8,128)(2,1)} %param.7) | copy-start | bytes 3145732
  16.8 8.1 %copy-start.1 = (bf16[128,4096]{1,0:T(8,128)(2,1)S(1)}, bf16[128,4096]{1,0:T(8,128)(2,1)}, u32[]{:S(2)}) copy-start(bf16[128,4096]{1,0:T(8,128)(2,1)} %param.8) | copy-start | bytes 3145732
  18.7 30.5 %all-to-all-start.1 = ((bf16[16,2,16384]{2,1,0:T(2,128)(2,1)}), bf16[16,2,16384]{2,1,0:T(2,128)(2,1)}, u32[]{:S(2)}, u32[]{:S(2)}) async-start(bf16[16,2,16384]{2,1,0:T(2,128)(2,1)} %reshape.316), calls=%async_computation.1 | async-start | bytes 2097152 | tf_op jit(solution)/shard_map/all_to_all | solution.py:103
  49.2 30.1 %all-to-all-start = ((bf16[16,2,16384]{2,1,0:T(2,128)(2,1)}), bf16[16,2,16384]{2,1,0:T(2,128)(2,1)}, u32[]{:S(2)}, u32[]{:S(2)}) async-start(bf16[16,2,16384]{2,1,0:T(2,128)(2,1)} %reshape.318), calls=%async_computation | async-start | bytes 2097152 | tf_op jit(solution)/shard_map/all_to_all | solution.py:100
  135.5 365.3 %all-to-all-start.2 = ((f32[2,32,8,8192]{3,2,0,1:T(8,128)}), f32[2,32,8,8192]{3,2,0,1:T(8,128)}, u32[]{:S(2)}, u32[]{:S(2)}) async-start(f32[2,32,8,8192]{3,2,0,1:T(8,128)} %pad_maximum_fusion), calls=%async_computation.2 | async-start | bytes 33554432 | tf_op jit(solution)/shard_map/all_to_all | solution.py:115
  554.0 97.6 %all-to-all-start.3 = ((bf16[2,2,128,4096]{3,0,1,2:T(2,128)(2,1)}), bf16[2,2,128,4096]{3,0,1,2:T(2,128)(2,1)}, u32[]{:S(2)}, u32[]{:S(2)}) async-start(bf16[2,2,128,4096]{3,0,1,2:T(2,128)(2,1)} %copy.34), calls=%async_computation.3 | async-start | bytes 8388608 | tf_op jit(solution)/shard_map/all_to_all | solution.py:120
  661.6 33.6 %copy-start.3 = (f32[4096]{0:T(1024)S(1)}, f32[4096]{0:T(1024)}, u32[]{:S(2)}) copy-start(f32[4096]{0:T(1024)} %param.11) | copy-start | bytes 49156
  663.2 32.0 %all-to-all-start.4 = ((bf16[16,8,4096]{2,1,0:T(8,128)(2,1)}), bf16[16,8,4096]{2,1,0:T(8,128)(2,1)}, u32[]{:S(2)}, u32[]{:S(2)}) async-start(bf16[16,8,4096]{2,1,0:T(8,128)(2,1)} %bitcast.63), calls=%async_computation.4 | async-start | bytes 2097152 | tf_op jit(solution)/shard_map/all_to_all | solution.py:124
where the time goes:
time: 707 us; the launch traced here: 699 us
  waiting for transfers between devices  500 us (71%)
  local copies, waits for them, and re-layouts  70.2 us (10%)
  other arithmetic  47.2 us (7%)
  matrix products  46.1 us (7%)
  starting transfers between devices  34.7 us (5%)
    all_to_all x1, waiting for transfers between devices, along_rows(): lax.all_to_all(spectra, 'seq', split_axis=1, concat_axis=2, tiled=True)  359 us
    all_to_all x1, waiting for transfers between devices, along_rows(): lax.all_to_all(joint.astype(jnp.bfloat16), 'seq', split_axis=2, concat_ax...  90.1 us
    unnamed x20, local copies, waits for them, and re-layouts  39.1 us
    dot_general x2, matrix products, row_transform(): return jnp.einsum('ymxn,xknc->ykmc', full_table, stacked, precision=PRECISE)  37.4 us
    all_to_all x1, waiting for transfers between devices, along_rows(): lax.all_to_all(convolved, 'seq', split_axis=0, concat_axis=1, tiled=True)  23.4 us
    all_to_all x1, waiting for transfers between devices, along_rows(): lax.all_to_all(product.reshape(1, row_count, channels), 'seq', split_axis...  18.2 us
    unnamed x2, other arithmetic  15 us
  transfers between devices with their start and end apart: 6, of which 5 were waited for; matrix products, arithmetic and copies ran while one was open for 5% of the time, Pallas kernels for 0%

commit v1 on v0

--- a/solution.py
+++ b/solution.py
@@ -5,6 +5,12 @@
 from jax.sharding import PartitionSpec as P
 
 PRECISE = lax.Precision.HIGHEST
+
+
+def stacked_exchange(shard, axis, split, join):
+    shards = jnp.split(shard, lax.axis_size(axis), axis=split)
+    arrived = lax.all_to_all(jnp.stack(shards), axis, 0, 0)
+    return jnp.concatenate(arrived, axis=join)
 
 
 def from_behind(value, axis, steps):
@@ -100,13 +106,7 @@
         lax.all_to_all(
             product.reshape(1, row_count, channels), "seq", split_axis=1, concat_axis=0, tiled=True
         ),
-        lax.all_to_all(
-            long_filter.reshape(1, row_count, channels),
-            "seq",
-            split_axis=1,
-            concat_axis=0,
-            tiled=True,
-        ),
+        stacked_exchange(long_filter.reshape(1, row_count, channels), "seq", 1, 0),
     )
     joined = jnp.concatenate([data_parts, kernel_parts], axis=2).astype(jnp.float32)
     freq_all = jnp.arange(2 * blocks, dtype=jnp.int32)

time: 707 us -> 728 us (1.030)
  local copies, waits for them, and re-layouts: 70.2 us -> 84.3 us
  waiting for transfers between devices: 500 us -> 511 us
    unnamed x20 -> x30, local copies, waits for them, and re-layouts: 39.1 us -> 53.8 us
    all_to_all x1, waiting for transfers between devices: 9.34 us -> 18.3 us  [stacked_exchange(): arrived = lax.all_to_all(jnp.stack(shards), axis, 0, 0)]
    unnamed x2 -> x1, other arithmetic: 15 us -> 8 us
where the time goes in v1:
time: 728 us; the launch traced here: 718 us
  waiting for transfers between devices  511 us (70%)
  local copies, waits for them, and re-layouts  84.3 us (12%)
  matrix products  46.1 us (6%)
  other arithmetic  41.8 us (6%)
  starting transfers between devices  33.9 us (5%)
    all_to_all x1, waiting for transfers between devices, along_rows(): lax.all_to_all(spectra, 'seq', split_axis=1, concat_axis=2, tiled=True)  359 us
    all_to_all x1, waiting for transfers between devices, along_rows(): lax.all_to_all(joint.astype(jnp.bfloat16), 'seq', split_axis=2, concat_ax...  90.1 us
    unnamed x30, local copies, waits for them, and re-layouts  53.8 us
    dot_general x2, matrix products, row_transform(): return jnp.einsum('ymxn,xknc->ykmc', full_table, stacked, precision=PRECISE)  37.4 us
    all_to_all x1, waiting for transfers between devices, along_rows(): lax.all_to_all(convolved, 'seq', split_axis=0, concat_axis=1, tiled=True)  23.4 us
    all_to_all x1, waiting for transfers between devices, along_rows(): lax.all_to_all(product.reshape(1, row_count, channels), 'seq', split_axis...  20.3 us
    all_to_all x1, waiting for transfers between devices, stacked_exchange(): arrived = lax.all_to_all(jnp.stack(shards), axis, 0, 0)  18.3 us
  transfers between devices with their start and end apart: 6, of which 5 were waited for; matrix products, arithmetic and copies ran while one was open for 5% of the time, Pallas kernels for 0%

profile of v1, /device:TPU:9, one launch (start us, length us, event | category | flops | bytes accessed | tf_op | source)
XLA Modules:
  0.0 717.7 jit_solution(12662536486576392163)
XLA Ops:
  0.0 0.9 slice_bitcast_fusion.21
  1.0 0.9 slice_bitcast_fusion.19
  2.0 3.7 collective-permute-start
  5.7 1.5 fusion.52
  7.1 1.5 fusion.51
  8.6 1.5 fusion.50
  10.1 1.5 fusion.49
  11.6 1.5 fusion.48
  13.0 1.5 fusion.47
  14.5 1.5 fusion.46
  16.0 1.5 fusion.45
  17.5 1.5 fusion.44
  18.9 1.5 fusion.43
  20.4 1.5 fusion.42
  21.9 1.5 fusion.41
  23.3 1.3 fusion.98
  24.6 1.5 fusion.40
  26.1 1.5 maximum_convert_fusion.1
  27.7 0.3 maximum_convert_fusion.2
  28.0 1.3 fusion.18
  29.3 2.4 copy.87
  31.7 0.5 broadcast.416
  32.2 8.0 %reduce = bf16[128,4096]{1,0:T(8,128)(2,1)} reduce(bf16[128,1,4096]{2,1,0:T(2,128)(2,1)S(1)} %bitcast.209, bf16[]{:T(256)} %broadcast.416), dimensions={1}, to_apply=%bitcast.197.reduce_sub_computation | reduce | bytes 2097154
  40.2 2.9 reshape.317
  43.2 5.4 all-to-all-start
  48.6 1.5 fusion.39
  50.0 1.5 fusion.38
  51.5 1.5 fusion.37
  53.0 20.3 %all-to-all-done = bf16[16,2,16384]{2,1,0:T(2,128)(2,1)S(1)} async-done(((bf16[16,2,16384]{2,1,0:T(2,128)(2,1)}), bf16[16,2,16384]{2,1,0:T(2,128)(2,1)S(1)}, u32[]{:S(2)}, u32[]{:S(2)}) %all-to-all-start) | async-done | bytes 1048608 | tf_op jit(solution)/shard_map/all_to_all | solution.py:106
  73.3 5.0 all-to-all-start.1
  78.4 4.3 reshape.318
  82.8 2.1 copy.86
  84.9 18.3 %all-to-all-done.1 = bf16[16,1,8,4096]{3,2,1,0:T(8,128)(2,1)} async-done(((bf16[16,1,8,4096]{3,2,1,0:T(8,128)(2,1)}), bf16[16,1,8,4096]{3,2,1,0:T(8,128)(2,1)}, u32[]{:S(2)}, u32[]{:S(2)}) %all-to-all-start.1) | async-done | bytes 1048608 | tf_op jit(solution)/shard_map/all_to_all | solution.py:12
  103.2 1.7 pad_maximum_fusion.2
  104.9 1.2 copy.70
  106.1 6.8 fusion.75
  112.9 6.6 fusion.97
  119.6 8.2 %copy.72 = f32[4,8,8,8192]{3,2,1,0:T(8,128)S(1)} copy(f32[4,8,8,8192]{3,1,2,0:T(8,128)} %bitcast.203) | data formatting | bytes 16777216
  127.8 8.2 %copy.71 = f32[4,8,8,8192]{3,2,1,0:T(8,128)S(1)} copy(f32[4,8,8,8192]{3,1,2,0:T(8,128)} %bitcast.202) | data formatting | bytes 16777216
  136.1 6.9 fusion.8
  143.0 11.5 %pad_maximum_fusion = f32[2,32,8,8192]{3,2,0,1:T(8,128)} fusion(f32[1,32,8,8192]{3,2,0,1:T(8,128)} %get-tuple-element.6, f32[1,32,8,8192]{3,2,0,1:T(8,128)} %get-tuple-element.5), kind=kLoop, calls=%fused_computation.2 | loop fusion | flops 4194304 | bytes 33554432 | tf_op jit(solution)/shard_map/stack | solution.py:58
  154.5 5.3 all-to-all-start.2
  159.8 0.3 fusion.59
  160.0 0.3 broadcast_multiply_fusion
  160.3 0.3 fusion.57
  160.6 0.1 fusion.92
  160.8 358.8 %all-to-all-done.2 = f32[2,32,8,8192]{3,2,0,1:T(8,128)} async-done(((f32[2,32,8,8192]{3,2,0,1:T(8,128)}), f32[2,32,8,8192]{3,2,0,1:T(8,128)}, u32[]{:S(2)}, u32[]{:S(2)}) %all-to-all-start.2) | async-done | bytes 16777248 | tf_op jit(solution)/shard_map/all_to_all | solution.py:115
  519.6 30.7 %fusion.3 = f32[2,2,128,8192]{2,3,0,1:T(8,128)S(1)} fusion(f32[1,128,2,128]{3,1,2,0:T(8,128)S(1)} %get-tuple-element.24, f32[1,128,2,128]{3,1,2,0:T(8,128)S(1)} %get-tuple-element.25, f32[2,2,16,8,8192]{4,3,0,1,2:T(8,128)} %bitcast.40), kind=kOutput, calls=%fused_computation.6 | convolution fusion | flops 12884967424 | bytes 33816576 | tf_op jit(solution)/shard_map/ymxn,xknc->ykmc/dot_general | solution.py:69
  550.3 1.1 multiply_subtract_fusion
  551.4 6.7 fusion.15
  558.1 1.1 add_convert_fusion
  559.2 2.4 pad_maximum_fusion.1
  561.6 11.2 %copy.59 = bf16[2,2,128,4096]{3,0,1,2:T(2,128)(2,1)} copy(bf16[2,2,128,4096]{2,3,0,1:T(8,128)(2,1)} %pad_maximum_fusion.1) | data formatting | bytes 8388608 | tf_op jit(solution)/shard_map/stack | solution.py:58
  572.9 7.5 %all-to-all-start.3 = ((bf16[2,2,128,4096]{3,0,1,2:T(2,128)(2,1)}), bf16[2,2,128,4096]{3,0,1,2:T(2,128)(2,1)}, u32[]{:S(2)}, u32[]{:S(2)}) async-start(bf16[2,2,128,4096]{3,0,1,2:T(2,128)(2,1)} %copy.59), calls=%async_computation.3 | async-start | bytes 8388608 | tf_op jit(solution)/shard_map/all_to_all | solution.py:120
  580.4 90.1 %all-to-all-done.3 = bf16[2,2,128,4096]{3,0,1,2:T(2,128)(2,1)} async-done(((bf16[2,2,128,4096]{3,0,1,2:T(2,128)(2,1)}), bf16[2,2,128,4096]{3,0,1,2:T(2,128)(2,1)}, u32[]{:S(2)}, u32[]{:S(2)}) %all-to-all-start.3) | async-done | bytes 4194336 | tf_op jit(solution)/shard_map/all_to_all | solution.py:120
  670.5 5.1 copy.85
  675.6 0.5 copy.61
  676.1 2.6 copy.73
  678.7 1.8 fusion
  680.5 1.5 copy.74
  682.1 7.1 all-to-all-start.4
  689.1 1.5 maximum_convert_fusion
  690.7 23.4 %all-to-all-done.4 = bf16[16,8,4096]{2,1,0:T(8,128)(2,1)} async-done(((bf16[16,8,4096]{2,1,0:T(8,128)(2,1)}), bf16[16,8,4096]{2,1,0:T(8,128)(2,1)}, u32[]{:S(2)}, u32[]{:S(2)}) %all-to-all-start.4) | async-done | bytes 1048608 | tf_op jit(solution)/shard_map/all_to_all | solution.py:124
  714.1 3.2 fusion.24
  (15 shorter events, 0.4 us)
Async XLA Ops:
  0.0 27.7 %copy-start.1 = (bf16[128,4096]{1,0:T(8,128)(2,1)S(1)}, bf16[128,4096]{1,0:T(8,128)(2,1)}, u32[]{:S(2)}) copy-start(bf16[128,4096]{1,0:T(8,128)(2,1)} %param.8) | copy-start | bytes 3145732
  2.0 24.1 %collective-permute-start = (bf16[3,2,4096]{2,1,0:T(2,128)(2,1)S(1)}, bf16[3,2,4096]{2,1,0:T(2,128)(2,1)S(1)}, u32[]{:S(2)}, u32[]{:S(2)}) collective-permute-start(bf16[3,2,4096]{2,1,0:T(2,128)(2,1)S(1)} %pad_maximum_fusion.7), channel_id=1, source_target_pairs={{0,1},{1,2},{2,3},{3,4},{4,5},{5,6},{6,7},{7,8},{8,9},{9,10},{10,1... | collective-permute-start | bytes 147464 | tf_op jit(solution)/shard_map/ppermute | solution.py:19
  43.2 30.1 %all-to-all-start = ((bf16[16,2,16384]{2,1,0:T(2,128)(2,1)}), bf16[16,2,16384]{2,1,0:T(2,128)(2,1)S(1)}, u32[]{:S(2)}, u32[]{:S(2)}) async-start(bf16[16,2,16384]{2,1,0:T(2,128)(2,1)} %reshape.317), calls=%async_computation | async-start | bytes 2097152 | tf_op jit(solution)/shard_map/all_to_all | solution.py:106
  73.3 5.0 copy-start
  73.3 29.9 %all-to-all-start.1 = ((bf16[16,1,8,4096]{3,2,1,0:T(8,128)(2,1)}), bf16[16,1,8,4096]{3,2,1,0:T(8,128)(2,1)}, u32[]{:S(2)}, u32[]{:S(2)}) async-start(bf16[16,1,8,4096]{3,2,1,0:T(8,128)(2,1)} %fusion.37), calls=%async_computation.1 | async-start | bytes 2097152 | tf_op jit(solution)/shard_map/all_to_all | solution.py:12
  154.5 365.1 %all-to-all-start.2 = ((f32[2,32,8,8192]{3,2,0,1:T(8,128)}), f32[2,32,8,8192]{3,2,0,1:T(8,128)}, u32[]{:S(2)}, u32[]{:S(2)}) async-start(f32[2,32,8,8192]{3,2,0,1:T(8,128)} %pad_maximum_fusion), calls=%async_computation.2 | async-start | bytes 33554432 | tf_op jit(solution)/shard_map/all_to_all | solution.py:115
  572.9 97.6 %all-to-all-start.3 = ((bf16[2,2,128,4096]{3,0,1,2:T(2,128)(2,1)}), bf16[2,2,128,4096]{3,0,1,2:T(2,128)(2,1)}, u32[]{:S(2)}, u32[]{:S(2)}) async-start(bf16[2,2,128,4096]{3,0,1,2:T(2,128)(2,1)} %copy.59), calls=%async_computation.3 | async-start | bytes 8388608 | tf_op jit(solution)/shard_map/all_to_all | solution.py:120
  680.5 33.6 %copy-start.2 = (f32[4096]{0:T(1024)S(1)}, f32[4096]{0:T(1024)}, u32[]{:S(2)}) copy-start(f32[4096]{0:T(1024)} %param.11) | copy-start | bytes 49156
  682.1 32.0 %all-to-all-start.4 = ((bf16[16,8,4096]{2,1,0:T(8,128)(2,1)}), bf16[16,8,4096]{2,1,0:T(8,128)(2,1)}, u32[]{:S(2)}, u32[]{:S(2)}) async-start(bf16[16,8,4096]{2,1,0:T(8,128)(2,1)} %bitcast.79), calls=%async_computation.4 | async-start | bytes 2097152 | tf_op jit(solution)/shard_map/all_to_all | solution.py:124
